TPU v7x, 32 devices: a whole 2x2x4 slice. The times are simulated.
32 devices in a mesh: grp: 2 (over y), seq: 4 (over z), sub: 4 (over x, core).
Axes of the slice: x: 2, y: 2, z: 4, core: 2. Of those that a mesh axis runs over, the one named last changes fastest.
Arguments:
- activations: bfloat16 [32768, 384], P(('grp', 'seq', 'sub')), parts along dimension 0, may hold values from -6 to 6
- cotangent: bfloat16 [32768, 384], P(('grp', 'seq', 'sub')), parts along dimension 0, may hold values from -6 to 6
- weights: bfloat16 [2304, 384], P('sub'), may hold values from -0.1875 to 0.1875
Outputs:
- input_grad: bfloat16 [32768, 384], P(('grp', 'seq', 'sub')), parts along dimension 0
- weight_grad: float32 [4608, 384], P(('grp', 'sub')), parts along dimension 0
There are 2 independent parts, one for each index of `grp`. A program takes and returns all parts, laid end to end along the dimension named above; an argument that names none is the same for every part. Nothing has to cross between parts.
All inputs are finite; a program needn't handle non-finite values.
Results may differ from a plain program's by a relative error of at most 0.0053.
Values may be sent and summed in bfloat16 or wider, within the bound.
No kernel may reach another device: no remote copies, remote signals or barrier semaphores. Data moves between devices by JAX's collectives and lax.ppermute only.
A program may use at most 64 MiB of HBM per device.

v0:
```python
import math
import jax
import jax.numpy as jnp
from jax import lax
from jax.sharding import PartitionSpec as P

DILATION_FIRST = 1024
DILATION_SECOND = 2048


def from_behind(block, axis, distance):
    devices = range(lax.axis_size(axis))
    route = [(i - distance, i) for i in devices if i - distance in devices]
    return lax.ppermute(block, axis, route)


def gelu_pair(pre_act):
    coeff = 0.7978845608
    tanh_value = jnp.tanh(coeff * (pre_act + 0.044715 * pre_act * pre_act * pre_act))
    gelu_value = 0.5 * pre_act * (1.0 + tanh_value)
    gelu_slope = 0.5 * (1.0 + tanh_value) + 0.5 * pre_act * (
        1.0 - tanh_value * tanh_value
    ) * coeff * (1.0 + 3.0 * 0.044715 * pre_act * pre_act)
    return (gelu_value, gelu_slope)


def back_product(spread, kernel, count_of_rows, channels):
    spread_three = spread.reshape(count_of_rows, 3, channels)
    kernel_three = kernel.reshape(3, channels, channels)
    return lax.dot_general(
        spread_three, kernel_three, (((1, 2), (0, 2)), ((), ())), preferred_element_type=jnp.float32
    )


def tap_grads(stacked, delta):
    return lax.dot_general(
        stacked, delta, (((0,), (0,)), ((), ())), preferred_element_type=jnp.float32
    )


def per_device(activations, cotangent, weights):
    count_of_rows, channels = activations.shape
    devices = lax.axis_size("seq") * lax.axis_size("sub")
    nearby_jumps = DILATION_FIRST // count_of_rows
    distant_jumps = DILATION_SECOND // count_of_rows
    grad_scale = 1.0 / math.sqrt(count_of_rows * devices)
    all_weights = lax.all_gather(weights, "sub", axis=0, tiled=True)
    first = all_weights[: 3 * channels]
    second = all_weights[3 * channels :]

    def near_rows(source, sign):
        return from_behind(source, ("seq", "sub"), sign * nearby_jumps)

    def far_rows(source, sign):
        return from_behind(source, ("seq", "sub"), sign * distant_jumps)

    first_layer_weights = jnp.concatenate(
        (near_rows(activations, 1), activations, near_rows(activations, -1)), 1
    )
    pre_one = jnp.dot(first_layer_weights, first, preferred_element_type=jnp.float32)
    gelu_one, slope_one = gelu_pair(pre_one)
    middle_state = (activations.astype(jnp.float32) + gelu_one).astype(jnp.bfloat16)
    second_layer_weights = jnp.concatenate(
        (far_rows(middle_state, 1), middle_state, far_rows(middle_state, -1)), 1
    )
    pre_two = jnp.dot(second_layer_weights, second, preferred_element_type=jnp.float32)
    gelu_two, slope_two = gelu_pair(pre_two)
    second_error = (cotangent.astype(jnp.float32) * slope_two).astype(jnp.bfloat16)
    grad_two = tap_grads(second_layer_weights, second_error) * grad_scale
    second_reach = jnp.concatenate(
        (far_rows(second_error, -1), second_error, far_rows(second_error, 1)), 1
    )
    back_one = cotangent.astype(jnp.float32) + back_product(
        second_reach, second, count_of_rows, channels
    )
    first_error = (back_one * slope_one).astype(jnp.bfloat16)
    grad_one = tap_grads(first_layer_weights, first_error) * grad_scale
    first_reach = jnp.concatenate(
        (near_rows(first_error, -1), first_error, near_rows(first_error, 1)), 1
    )
    input_grad = (back_one + back_product(first_reach, first, count_of_rows, channels)).astype(
        jnp.bfloat16
    )
    local_grads = jnp.concatenate((grad_one, grad_two), 0)
    summed = lax.psum(local_grads, "seq")
    weight_grad = lax.psum_scatter(summed, "sub", scatter_dimension=0, tiled=True)
    return (input_grad, weight_grad)


def solution(mesh):
    placed = (P(("grp", "seq", "sub"), None), P(("grp", "seq", "sub"), None), P("sub", None))
    return jax.shard_map(
        per_device,
        mesh=mesh,
        in_specs=placed,
        out_specs=(P(("grp", "seq", "sub"), None), P(("grp", "sub"), None)),
        check_vma=False,
    )
```

profile of v0, /device:TPU:0, one launch (start us, length us, event | category | flops | bytes accessed | tf_op | source)
XLA Modules:
  0.0 237.5 jit_solution(14820011768576403430)
XLA Ops:
  8.0 2.4 %collective-permute-start = (bf16[1024,384]{1,0:T(8,128)(2,1)}, bf16[1024,384]{1,0:T(8,128)(2,1)S(1)}, u32[]{:S(2)}, u32[]{:S(2)}) collective-permute-start(bf16[1024,384]{1,0:T(8,128)(2,1)} %param.3), channel_id=1, source_target_pairs={{0,1},{1,2},{2,3},{3,4},{4,5},{5,6},{6,7},{7,8},{8,9},{9,10},{10,1... | collective-permute-start | bytes 2359304 | tf_op jit(solution)/shard_map/ppermute | solution.py:14
  10.4 1.3 collective-permute-start.1
  11.7 1.4 copy.6
  15.1 1.7 collective-permute-done.1
  17.8 22.2 %all-gather.2.cloned.1.call-done = bf16[2304,384]{1,0:T(8,128)(2,1)} async-done(((bf16[576,384]{1,0:T(8,128)(2,1)}), bf16[2304,384]{1,0:T(8,128)(2,1)}) %all-gather.2.cloned.1.call-update) | async-done | bytes 1769488 | tf_op jit(solution)/shard_map/all_gather | solution.py:47
  40.0 4.9 %add_convert_fusion = (bf16[1024,384]{0,1:T(8,128)(2,1)}, f32[1024,384]{0,1:T(8,128)}) fusion(bf16[1024,384]{0,1:T(8,128)(2,1)S(1)} %copy.6, bf16[1024,1152]{1,0:T(8,128)(2,1)} %constant_dynamic-update-slice_fusion, bf16[2304,384]{1,0:T(8,128)(2,1)} %all-gather.2.cloned.1.call-done), kind=kOutput, calls=%fused_computation.27 | convolution fusion | flops 910295040 | bytes 6389760 | tf_op jit(solution)/shard_map/dot_general | solution.py:60
  44.9 1.3 collective-permute-start.3
  46.2 7.3 %collective-permute-start.2 = (bf16[1024,384]{0,1:T(8,128)(2,1)}, bf16[1024,384]{0,1:T(8,128)(2,1)}, u32[]{:S(2)}, u32[]{:S(2)}) collective-permute-start(bf16[1024,384]{0,1:T(8,128)(2,1)} %get-tuple-element.6), channel_id=1, source_target_pairs={{0,2},{1,3},{2,4},{3,5},{4,6},{5,7},{6,8},{7,9},{8,10},{9,11},{10,... | collective-permute-start | bytes 2359304 | tf_op jit(solution)/shard_map/ppermute | solution.py:14
  53.8 15.1 %collective-permute-done.3 = bf16[1024,384]{0,1:T(8,128)(2,1)} collective-permute-done((bf16[1024,384]{0,1:T(8,128)(2,1)}, bf16[1024,384]{0,1:T(8,128)(2,1)}, u32[]{:S(2)}, u32[]{:S(2)}) %collective-permute-start.3) | collective-permute-done | bytes 786464 | tf_op jit(solution)/shard_map/ppermute | solution.py:14
  68.9 17.0 %collective-permute-done.2 = bf16[1024,384]{0,1:T(8,128)(2,1)} collective-permute-done((bf16[1024,384]{0,1:T(8,128)(2,1)}, bf16[1024,384]{0,1:T(8,128)(2,1)}, u32[]{:S(2)}, u32[]{:S(2)}) %collective-permute-start.2) | collective-permute-done | bytes 786464 | tf_op jit(solution)/shard_map/ppermute | solution.py:14
  85.9 3.7 %fusion = bf16[1024,384]{0,1:T(8,128)(2,1)S(1)} fusion(bf16[1024,384]{0,1:T(8,128)(2,1)S(1)} %copy.5, bf16[1024,384]{0,1:T(8,128)(2,1)} %collective-permute-done.3, bf16[1024,384]{0,1:T(8,128)(2,1)} %get-tuple-element.6, bf16[1024,384]{0,1:T(8,128)(2,1)} %collective-permute-done.2, bf16[2304,384]{1,0:T(8,128)(2,1)S(1)} %copy-done.1), kind=kOutput, calls=%fused_computation.12 | convolution fusion | flops 920911872 | bytes 4816896 | tf_op jit(solution)/shard_map/dot_general | solution.py:66
  89.6 4.4 %collective-permute-start.5 = (bf16[1024,384]{0,1:T(8,128)(2,1)S(1)}, bf16[1024,384]{0,1:T(8,128)(2,1)S(1)}, u32[]{:S(2)}, u32[]{:S(2)}) collective-permute-start(bf16[1024,384]{0,1:T(8,128)(2,1)S(1)} %fusion), channel_id=1, source_target_pairs={{0,2},{1,3},{2,4},{3,5},{4,6},{5,7},{6,8},{7,9},{8,10},{9,11},{10,... | collective-permute-start | bytes 2359304 | tf_op jit(solution)/shard_map/ppermute | solution.py:14
  94.0 1.3 collective-permute-start.4
  95.5 3.0 %convolution_multiply_fusion = f32[1152,384]{1,0:T(8,128)S(1)} fusion(bf16[1024,384]{0,1:T(8,128)(2,1)S(1)} %fusion, bf16[1024,384]{0,1:T(8,128)(2,1)} %collective-permute-done.3, bf16[1024,384]{0,1:T(8,128)(2,1)} %get-tuple-element.6, bf16[1024,384]{0,1:T(8,128)(2,1)} %collective-permute-done.2), kind=kOutput, calls=%fused_computation.1 | convolution fusion | flops 913489920 | bytes 4915200 | tf_op jit(solution)/shard_map/dot_general | solution.py:36
  98.6 29.3 %collective-permute-done.5 = bf16[1024,384]{0,1:T(8,128)(2,1)S(1)} collective-permute-done((bf16[1024,384]{0,1:T(8,128)(2,1)S(1)}, bf16[1024,384]{0,1:T(8,128)(2,1)S(1)}, u32[]{:S(2)}, u32[]{:S(2)}) %collective-permute-start.5) | collective-permute-done | bytes 786464 | tf_op jit(solution)/shard_map/ppermute | solution.py:14
  128.1 3.0 %fusion.12 = (bf16[1024,384]{0,1:T(8,128)(2,1)S(1)}, f32[1024,384]{0,1:T(8,128)}) fusion(f32[1024,384]{0,1:T(8,128)S(1)} %copy-done.4, bf16[3,384,384]{2,1,0:T(8,128)(2,1)S(1)} %bitcast.21, bf16[1024,3,384]{0,2,1:T(8,128)(2,1)S(1)} %bitcast.18, bf16[1024,384]{0,1:T(8,128)(2,1)S(1)} %copy.5), kind=kOutput, calls=%fused_computation.24 | convolution fusion | flops 914227200 | bytes 7962624 | tf_op jit(solution)/shard_map/dot_general | solution.py:30
  131.1 3.1 %convolution_multiply_fusion.1 = f32[1152,384]{1,0:T(8,128)S(1)} fusion(bf16[1024,1152]{1,0:T(8,128)(2,1)} %constant_dynamic-update-slice_fusion, bf16[1024,384]{0,1:T(8,128)(2,1)S(1)} %get-tuple-element.8), kind=kOutput, calls=%fused_computation.2 | convolution fusion | flops 906412032 | bytes 4915200 | tf_op jit(solution)/shard_map/dot_general | solution.py:36
  134.2 2.0 pad_maximum_fusion
  136.3 1.3 collective-permute-start.7
  137.6 1.3 collective-permute-start.6
  138.9 39.1 %reduce-scatter.2.cloned.1.call-done = f32[576,384]{1,0:T(8,128)} async-done(((f32[2304,384]{1,0:T(8,128)}), f32[576,384]{1,0:T(8,128)}) %reduce-scatter.2.cloned.1.call-update) | async-done | bytes 884752 | tf_op jit(solution)/shard_map/reduce_scatter | solution.py:86
  179.5 1.2 fusion.13
  181.8 47.0 %all-reduce.2.cloned.1.call-done = f32[576,384]{1,0:T(8,128)} async-done(((f32[576,384]{1,0:T(8,128)}), f32[576,384]{1,0:T(8,128)}) %all-reduce.2.cloned.1.call-update) | async-done | bytes 884752 | tf_op jit(solution)/shard_map/psum | solution.py:85
  228.8 2.1 copy.18
  (28 shorter events, 7.0 us)
Async XLA Ops:
  7.2 6.9 %copy-start = (bf16[1024,384]{1,0:T(8,128)(2,1)S(1)}, bf16[1024,384]{1,0:T(8,128)(2,1)}, u32[]{:S(2)}) copy-start(bf16[1024,384]{1,0:T(8,128)(2,1)} %param.3) | copy-start | bytes 2359300
  7.2 32.8 %all-gather.2.cloned.1.call-start = ((), (), s32[]{:S(2)}) async-start(), calls=%async_computation.1 | async-start | bytes 2211840 | tf_op jit(solution)/shard_map/all_gather | solution.py:47
  7.9 170.1 %reduce-scatter.2.cloned.1.call-start = ((), (), s32[]{:S(2)}) async-start(), calls=%async_computation.2 | async-start | bytes 4423680 | tf_op jit(solution)/shard_map/reduce_scatter | solution.py:86
  8.0 5.1 %collective-permute-start = (bf16[1024,384]{1,0:T(8,128)(2,1)}, bf16[1024,384]{1,0:T(8,128)(2,1)S(1)}, u32[]{:S(2)}, u32[]{:S(2)}) collective-permute-start(bf16[1024,384]{1,0:T(8,128)(2,1)} %param.3), channel_id=1, source_target_pairs={{0,1},{1,2},{2,3},{3,4},{4,5},{5,6},{6,7},{7,8},{8,9},{9,10},{10,1... | collective-permute-start | bytes 2359304 | tf_op jit(solution)/shard_map/ppermute | solution.py:14
  10.4 6.4 %collective-permute-start.1 = (bf16[1024,384]{1,0:T(8,128)(2,1)}, bf16[1024,384]{1,0:T(8,128)(2,1)S(1)}, u32[]{:S(2)}, u32[]{:S(2)}) collective-permute-start(bf16[1024,384]{1,0:T(8,128)(2,1)} %param.3), channel_id=1, source_target_pairs={{1,0},{2,1},{3,2},{4,3},{5,4},{6,5},{7,6},{8,7},{9,8},{10,9},{11,1... | collective-permute-start | bytes 2359304 | tf_op jit(solution)/shard_map/ppermute | solution.py:14
  17.8 35.7 %copy-start.2 = (bf16[1024,384]{1,0:T(8,128)(2,1)S(1)}, bf16[1024,384]{1,0:T(8,128)(2,1)}, u32[]{:S(2)}) copy-start(bf16[1024,384]{1,0:T(8,128)(2,1)} %param.4) | copy-start | bytes 2359300
  40.0 46.0 %copy-start.1 = (bf16[2304,384]{1,0:T(8,128)(2,1)S(1)}, bf16[2304,384]{1,0:T(8,128)(2,1)}, u32[]{:S(2)}) copy-start(bf16[2304,384]{1,0:T(8,128)(2,1)} %all-gather.2.cloned.1.call-done) | copy-start | bytes 5308420
  44.9 24.0 %collective-permute-start.3 = (bf16[1024,384]{0,1:T(8,128)(2,1)}, bf16[1024,384]{0,1:T(8,128)(2,1)}, u32[]{:S(2)}, u32[]{:S(2)}) collective-permute-start(bf16[1024,384]{0,1:T(8,128)(2,1)} %get-tuple-element.6), channel_id=1, source_target_pairs={{2,0},{3,1},{4,2},{5,3},{6,4},{7,5},{8,6},{9,7},{10,8},{11,9},{12,... | collective-permute-start | bytes 2359304 | tf_op jit(solution)/shard_map/ppermute | solution.py:14
  46.2 39.7 %collective-permute-start.2 = (bf16[1024,384]{0,1:T(8,128)(2,1)}, bf16[1024,384]{0,1:T(8,128)(2,1)}, u32[]{:S(2)}, u32[]{:S(2)}) collective-permute-start(bf16[1024,384]{0,1:T(8,128)(2,1)} %get-tuple-element.6), channel_id=1, source_target_pairs={{0,2},{1,3},{2,4},{3,5},{4,6},{5,7},{6,8},{7,9},{8,10},{9,11},{10,... | collective-permute-start | bytes 2359304 | tf_op jit(solution)/shard_map/ppermute | solution.py:14
  89.6 38.2 %collective-permute-start.5 = (bf16[1024,384]{0,1:T(8,128)(2,1)S(1)}, bf16[1024,384]{0,1:T(8,128)(2,1)S(1)}, u32[]{:S(2)}, u32[]{:S(2)}) collective-permute-start(bf16[1024,384]{0,1:T(8,128)(2,1)S(1)} %fusion), channel_id=1, source_target_pairs={{0,2},{1,3},{2,4},{3,5},{4,6},{5,7},{6,8},{7,9},{8,10},{9,11},{10,... | collective-permute-start | bytes 2359304 | tf_op jit(solution)/shard_map/ppermute | solution.py:14
  94.0 33.8 %collective-permute-start.4 = (bf16[1024,384]{0,1:T(8,128)(2,1)S(1)}, bf16[1024,384]{0,1:T(8,128)(2,1)S(1)}, u32[]{:S(2)}, u32[]{:S(2)}) collective-permute-start(bf16[1024,384]{0,1:T(8,128)(2,1)S(1)} %fusion), channel_id=1, source_target_pairs={{2,0},{3,1},{4,2},{5,3},{6,4},{7,5},{8,6},{9,7},{10,8},{11,9},{12,... | collective-permute-start | bytes 2359304 | tf_op jit(solution)/shard_map/ppermute | solution.py:14
  98.6 29.5 %copy-start.4 = (f32[1024,384]{0,1:T(8,128)S(1)}, f32[1024,384]{0,1:T(8,128)}, u32[]{:S(2)}) copy-start(f32[1024,384]{0,1:T(8,128)} %get-tuple-element.7) | copy-start | bytes 4718596
  136.2 92.6 %all-reduce.2.cloned.1.call-start = ((), (), s32[]{:S(2)}) async-start(), calls=%async_computation.3 | async-start | bytes 1769472 | tf_op jit(solution)/shard_map/psum | solution.py:85
  136.3 41.8 %collective-permute-start.7 = (bf16[1024,384]{0,1:T(8,128)(2,1)S(1)}, bf16[1024,384]{0,1:T(8,128)(2,1)S(1)}, u32[]{:S(2)}, u32[]{:S(2)}) collective-permute-start(bf16[1024,384]{0,1:T(8,128)(2,1)S(1)} %get-tuple-element.8), channel_id=1, source_target_pairs={{0,1},{1,2},{2,3},{3,4},{4,5},{5,6},{6,7},{7,8},{8,9},{9,10},{10,1... | collective-permute-start | bytes 2359304 | tf_op jit(solution)/shard_map/ppermute | solution.py:14
  137.6 40.5 %collective-permute-start.6 = (bf16[1024,384]{0,1:T(8,128)(2,1)S(1)}, bf16[1024,384]{0,1:T(8,128)(2,1)S(1)}, u32[]{:S(2)}, u32[]{:S(2)}) collective-permute-start(bf16[1024,384]{0,1:T(8,128)(2,1)S(1)} %get-tuple-element.8), channel_id=1, source_target_pairs={{1,0},{2,1},{3,2},{4,3},{5,4},{6,5},{7,6},{8,7},{9,8},{10,9},{11,1... | collective-permute-start | bytes 2359304 | tf_op jit(solution)/shard_map/ppermute | solution.py:14
  178.1 1.4 copy-start.3
Sparse Core Ops, SparseCore 0:
  9.6 30.3 all-gather.1
  136.3 41.6 reduce-scatter.1
  180.5 48.2 all-reduce.1
where the time goes:
time: 238 us; the launch traced here: 237 us
  waiting for transfers between devices  172 us (72%)
  starting transfers between devices  20.8 us (9%)
  matrix products  18.9 us (8%)
  between operations  13.9 us (6%)
  local copies, waits for them, and re-layouts  9.33 us (4%)
  other arithmetic  2.4 us (1%)
    ppermute x8, waiting for transfers between devices, from_behind(): return lax.ppermute(block, axis, route)  63.1 us
    psum x1, waiting for transfers between devices, per_device(): summed = lax.psum(local_grads, 'seq')  47 us
    reduce_scatter x1, waiting for transfers between devices, per_device(): lax.psum_scatter(summed, 'sub', scatter_dimension=0, tiled=True)  39.1 us
    all_gather x1, waiting for transfers between devices, per_device(): all_weights = lax.all_gather(weights, 'sub', axis=0, tiled=True)  22.2 us
    ppermute x8, starting transfers between devices, from_behind(): return lax.ppermute(block, axis, route)  20.7 us
    unnamed x16, local copies, waits for them, and re-layouts  8.17 us
    dot_general x2, matrix products, tap_grads(): lax.dot_general(stacked, delta, (((0,), (0,)), ((), ())), preferred_eleme...  6.12 us
    dot_general x1, matrix products, per_device(): jnp.dot(first_layer_weights, first, preferred_element_type=jnp.float32)  4.94 us
  transfers between devices with their start and end apart: 11, of which 7 were waited for; matrix products, arithmetic and copies ran while one was open for 4% of the time, Pallas kernels for 0%

commit v1 on v0

--- a/solution.py
+++ b/solution.py
@@ -44,7 +44,12 @@
     nearby_jumps = DILATION_FIRST // count_of_rows
     distant_jumps = DILATION_SECOND // count_of_rows
     grad_scale = 1.0 / math.sqrt(count_of_rows * devices)
-    all_weights = lax.all_gather(weights, "sub", axis=0, tiled=True)
+    ring = [weights]
+    for hop in range(3):
+        ring.append(lax.ppermute(ring[-1], "sub", [(dev, (dev + 1) % 4) for dev in range(4)]))
+    all_weights = jnp.roll(
+        jnp.concatenate(ring[::-1], axis=0), (lax.axis_index("sub") + 1) * ring[0].shape[0], axis=0
+    )
     first = all_weights[: 3 * channels]
     second = all_weights[3 * channels :]
 

time: 238 us -> 238 us (level)
  starting transfers between devices: 20.8 us -> 35 us
  waiting for transfers between devices: 172 us -> 159 us
  matrix products: 18.9 us -> 15.3 us
    all_gather x1 -> x0, waiting for transfers between devices: 22.2 us -> none  [per_device(): all_weights = lax.all_gather(weights, 'sub', axis=0, tiled=True)]
    ppermute x0 -> x3, waiting for transfers between devices: none -> 13.9 us  [per_device(): lax.ppermute(ring[-1], 'sub', [(dev, (dev + 1) % 4) for dev in range(4)])]
    ppermute x0 -> x3, starting transfers between devices: none -> 9.58 us  [per_device(): lax.ppermute(ring[-1], 'sub', [(dev, (dev + 1) % 4) for dev in range(4)])]
    ppermute x8, starting transfers between devices: 20.7 us -> 25.4 us  [from_behind(): return lax.ppermute(block, axis, route)]
    ppermute x8, waiting for transfers between devices: 63.1 us -> 59.4 us  [from_behind(): return lax.ppermute(block, axis, route)]
    unnamed x16 -> x29, local copies, waits for them, and re-layouts: 8.17 us -> 10.1 us
  transfers between devices with their start and end apart: 11 -> 13, of which waited for: 7 -> 7; matrix products, arithmetic and copies ran while one was open for 4% -> 4% of each run, Pallas kernels for 0% -> 0%
where the time goes in v1:
time: 238 us; the launch traced here: 237 us
  waiting for transfers between devices  159 us (67%)
  starting transfers between devices  35 us (15%)
  matrix products  15.3 us (6%)
  between operations  14.3 us (6%)
  local copies, waits for them, and re-layouts  10.8 us (5%)
  other arithmetic  2.4 us (1%)
    ppermute x8, waiting for transfers between devices, from_behind(): return lax.ppermute(block, axis, route)  59.4 us
    psum x1, waiting for transfers between devices, per_device(): summed = lax.psum(local_grads, 'seq')  47 us
    reduce_scatter x1, waiting for transfers between devices, per_device(): lax.psum_scatter(summed, 'sub', scatter_dimension=0, tiled=True)  39.2 us
    ppermute x8, starting transfers between devices, from_behind(): return lax.ppermute(block, axis, route)  25.4 us
    ppermute x3, waiting for transfers between devices, per_device(): lax.ppermute(ring[-1], 'sub', [(dev, (dev + 1) % 4) for dev in range(4)])  13.9 us
    unnamed x29, local copies, waits for them, and re-layouts  10.1 us
    ppermute x3, starting transfers between devices, per_device(): lax.ppermute(ring[-1], 'sub', [(dev, (dev + 1) % 4) for dev in range(4)])  9.58 us
  transfers between devices with their start and end apart: 13, of which 7 were waited for; matrix products, arithmetic and copies ran while one was open for 4% of the time, Pallas kernels for 0%

profile of v1, /device:TPU:0, one launch (start us, length us, event | category | flops | bytes accessed | tf_op | source)
XLA Modules:
  0.0 237.4 jit_solution(10314840016827278539)
XLA Ops:
  7.7 5.4 %collective-permute-start = (bf16[1024,384]{1,0:T(8,128)(2,1)}, bf16[1024,384]{1,0:T(8,128)(2,1)}, u32[]{:S(2)}, u32[]{:S(2)}) collective-permute-start(bf16[1024,384]{1,0:T(8,128)(2,1)} %param.3), channel_id=1, source_target_pairs={{0,1},{1,2},{2,3},{3,4},{4,5},{5,6},{6,7},{7,8},{8,9},{9,10},{10,1... | collective-permute-start | bytes 2359304 | tf_op jit(solution)/shard_map/ppermute | solution.py:14
  13.1 1.3 collective-permute-start.1
  14.4 1.4 collective-permute-done.2
  15.9 12.4 %collective-permute-done.3 = bf16[576,384]{1,0:T(8,128)(2,1)S(1)} collective-permute-done((bf16[576,384]{1,0:T(8,128)(2,1)S(1)}, bf16[576,384]{1,0:T(8,128)(2,1)S(1)}, u32[]{:S(2)}, u32[]{:S(2)}) %collective-permute-start.3) | collective-permute-done | bytes 442400 | tf_op jit(solution)/shard_map/ppermute | solution.py:49
  28.3 9.0 %collective-permute-start.4 = (bf16[576,384]{1,0:T(8,128)(2,1)S(1)}, bf16[576,384]{1,0:T(8,128)(2,1)S(1)}, u32[]{:S(2)}, u32[]{:S(2)}) collective-permute-start(bf16[576,384]{1,0:T(8,128)(2,1)S(1)} %collective-permute-done.3), channel_id=1, source_target_pairs={{0,1},{1,2},{2,3},{3,0},{4,5},{5,6},{6,7},{7,4},{8,9},{9,10},{10,1... | collective-permute-start | bytes 1327112 | tf_op jit(solution)/shard_map/ppermute | solution.py:49
  37.4 2.3 copy.6
  43.5 3.0 %add_convert_fusion = (bf16[1024,384]{0,1:T(8,128)(2,1)}, f32[1024,384]{0,1:T(8,128)}) fusion(bf16[1024,384]{0,1:T(8,128)(2,1)S(1)} %copy-done.3, bf16[1024,1152]{1,0:T(8,128)(2,1)S(1)} %constant_dynamic-update-slice_fusion.8, bf16[1152,384]{1,0:T(8,128)(2,1)S(1)} %get-tuple-element.4), kind=kOutput, calls=%fused_computation.27 | convolution fusion | flops 910295040 | bytes 6389760 | tf_op jit(solution)/shard_map/dot_general | solution.py:65
  46.5 1.3 collective-permute-start.6
  47.8 9.1 %collective-permute-start.5 = (bf16[1024,384]{0,1:T(8,128)(2,1)}, bf16[1024,384]{0,1:T(8,128)(2,1)}, u32[]{:S(2)}, u32[]{:S(2)}) collective-permute-start(bf16[1024,384]{0,1:T(8,128)(2,1)} %get-tuple-element.6), channel_id=1, source_target_pairs={{0,2},{1,3},{2,4},{3,5},{4,6},{5,7},{6,8},{7,9},{8,10},{9,11},{10,... | collective-permute-start | bytes 2359304 | tf_op jit(solution)/shard_map/ppermute | solution.py:14
  57.1 14.3 %collective-permute-done.6 = bf16[1024,384]{0,1:T(8,128)(2,1)} collective-permute-done((bf16[1024,384]{0,1:T(8,128)(2,1)}, bf16[1024,384]{0,1:T(8,128)(2,1)}, u32[]{:S(2)}, u32[]{:S(2)}) %collective-permute-start.6) | collective-permute-done | bytes 786464 | tf_op jit(solution)/shard_map/ppermute | solution.py:14
  71.4 15.7 %collective-permute-done.5 = bf16[1024,384]{0,1:T(8,128)(2,1)} collective-permute-done((bf16[1024,384]{0,1:T(8,128)(2,1)}, bf16[1024,384]{0,1:T(8,128)(2,1)}, u32[]{:S(2)}, u32[]{:S(2)}) %collective-permute-start.5) | collective-permute-done | bytes 786464 | tf_op jit(solution)/shard_map/ppermute | solution.py:14
  87.1 3.7 %fusion = bf16[1024,384]{0,1:T(8,128)(2,1)S(1)} fusion(bf16[1024,384]{0,1:T(8,128)(2,1)S(1)} %copy.5, bf16[1152,384]{1,0:T(8,128)(2,1)S(1)} %get-tuple-element.5, bf16[1024,384]{0,1:T(8,128)(2,1)} %collective-permute-done.6, bf16[1024,384]{0,1:T(8,128)(2,1)} %get-tuple-element.6, bf16[1024,384]{0,1:T(8,128)(2,1)} %collective-permute-done.5), kind=kOutput, calls=%fused_computation.12 | convolution fusion | flops 920911872 | bytes 4816896 | tf_op jit(solution)/shard_map/dot_general | solution.py:71
  90.7 4.4 %collective-permute-start.8 = (bf16[1024,384]{0,1:T(8,128)(2,1)S(1)}, bf16[1024,384]{0,1:T(8,128)(2,1)S(1)}, u32[]{:S(2)}, u32[]{:S(2)}) collective-permute-start(bf16[1024,384]{0,1:T(8,128)(2,1)S(1)} %fusion), channel_id=1, source_target_pairs={{0,2},{1,3},{2,4},{3,5},{4,6},{5,7},{6,8},{7,9},{8,10},{9,11},{10,... | collective-permute-start | bytes 2359304 | tf_op jit(solution)/shard_map/ppermute | solution.py:14
  95.2 1.3 collective-permute-start.7
  96.5 3.0 %convolution_multiply_fusion = f32[1152,384]{1,0:T(8,128)S(1)} fusion(bf16[1024,384]{0,1:T(8,128)(2,1)S(1)} %fusion, bf16[1024,384]{0,1:T(8,128)(2,1)} %collective-permute-done.6, bf16[1024,384]{0,1:T(8,128)(2,1)} %get-tuple-element.6, bf16[1024,384]{0,1:T(8,128)(2,1)} %collective-permute-done.5), kind=kOutput, calls=%fused_computation.1 | convolution fusion | flops 913489920 | bytes 4915200 | tf_op jit(solution)/shard_map/dot_general | solution.py:36
  99.5 29.4 %collective-permute-done.8 = bf16[1024,384]{0,1:T(8,128)(2,1)S(1)} collective-permute-done((bf16[1024,384]{0,1:T(8,128)(2,1)S(1)}, bf16[1024,384]{0,1:T(8,128)(2,1)S(1)}, u32[]{:S(2)}, u32[]{:S(2)}) %collective-permute-start.8) | collective-permute-done | bytes 786464 | tf_op jit(solution)/shard_map/ppermute | solution.py:14
  129.2 3.1 %fusion.12 = (bf16[1024,384]{0,1:T(8,128)(2,1)S(1)}, f32[1024,384]{0,1:T(8,128)}) fusion(f32[1024,384]{0,1:T(8,128)S(1)} %copy-done.7, bf16[3,384,384]{2,1,0:T(8,128)(2,1)S(1)} %bitcast.23, bf16[1024,3,384]{0,2,1:T(8,128)(2,1)S(1)} %bitcast.20, bf16[1024,384]{0,1:T(8,128)(2,1)S(1)} %copy.5), kind=kOutput, calls=%fused_computation.24 | convolution fusion | flops 914227200 | bytes 7962624 | tf_op jit(solution)/shard_map/dot_general | solution.py:30
  132.3 1.4 convolution_multiply_fusion.1
  133.7 2.0 pad_maximum_fusion
  135.8 1.3 collective-permute-start.10
  137.1 1.3 collective-permute-start.9
  138.4 39.2 %reduce-scatter.2.cloned.1.call-done = f32[576,384]{1,0:T(8,128)} async-done(((f32[2304,384]{1,0:T(8,128)}), f32[576,384]{1,0:T(8,128)}) %reduce-scatter.2.cloned.1.call-update) | async-done | bytes 884752 | tf_op jit(solution)/shard_map/reduce_scatter | solution.py:91
  181.4 47.0 %all-reduce.2.cloned.1.call-done = f32[576,384]{1,0:T(8,128)} async-done(((f32[576,384]{1,0:T(8,128)}), f32[576,384]{1,0:T(8,128)}) %all-reduce.2.cloned.1.call-update) | async-done | bytes 884752 | tf_op jit(solution)/shard_map/psum | solution.py:90
  228.4 2.1 copy.25
  (45 shorter events, 8.6 us)
Async XLA Ops:
  7.2 33.7 %copy-start = (bf16[1024,384]{1,0:T(8,128)(2,1)S(1)}, bf16[1024,384]{1,0:T(8,128)(2,1)}, u32[]{:S(2)}) copy-start(bf16[1024,384]{1,0:T(8,128)(2,1)} %param.3) | copy-start | bytes 2359300
  7.2 170.4 %reduce-scatter.2.cloned.1.call-start = ((), (), s32[]{:S(2)}) async-start(), calls=%async_computation.1 | async-start | bytes 4423680 | tf_op jit(solution)/shard_map/reduce_scatter | solution.py:91
  7.2 8.6 %collective-permute-start.2 = (bf16[576,384]{1,0:T(8,128)(2,1)}, bf16[576,384]{1,0:T(8,128)(2,1)S(1)}, u32[]{:S(2)}, u32[]{:S(2)}) collective-permute-start(bf16[576,384]{1,0:T(8,128)(2,1)} %param.5), channel_id=1, source_target_pairs={{0,1},{1,2},{2,3},{3,0},{4,5},{5,6},{6,7},{7,4},{8,9},{9,10},{10,1... | collective-permute-start | bytes 1327112 | tf_op jit(solution)/shard_map/ppermute | solution.py:49
  7.7 31.9 %collective-permute-start = (bf16[1024,384]{1,0:T(8,128)(2,1)}, bf16[1024,384]{1,0:T(8,128)(2,1)}, u32[]{:S(2)}, u32[]{:S(2)}) collective-permute-start(bf16[1024,384]{1,0:T(8,128)(2,1)} %param.3), channel_id=1, source_target_pairs={{0,1},{1,2},{2,3},{3,4},{4,5},{5,6},{6,7},{7,8},{8,9},{9,10},{10,1... | collective-permute-start | bytes 2359304 | tf_op jit(solution)/shard_map/ppermute | solution.py:14
  13.1 28.0 %collective-permute-start.1 = (bf16[1024,384]{1,0:T(8,128)(2,1)}, bf16[1024,384]{1,0:T(8,128)(2,1)S(1)}, u32[]{:S(2)}, u32[]{:S(2)}) collective-permute-start(bf16[1024,384]{1,0:T(8,128)(2,1)} %param.3), channel_id=1, source_target_pairs={{1,0},{2,1},{3,2},{4,3},{5,4},{6,5},{7,6},{8,7},{9,8},{10,9},{11,1... | collective-permute-start | bytes 2359304 | tf_op jit(solution)/shard_map/ppermute | solution.py:14
  15.8 12.5 %collective-permute-start.3 = (bf16[576,384]{1,0:T(8,128)(2,1)S(1)}, bf16[576,384]{1,0:T(8,128)(2,1)S(1)}, u32[]{:S(2)}, u32[]{:S(2)}) collective-permute-start(bf16[576,384]{1,0:T(8,128)(2,1)S(1)} %collective-permute-done.2), channel_id=1, source_target_pairs={{0,1},{1,2},{2,3},{3,0},{4,5},{5,6},{6,7},{7,4},{8,9},{9,10},{10,1... | collective-permute-start | bytes 1327112 | tf_op jit(solution)/shard_map/ppermute | solution.py:49
  28.3 12.9 %collective-permute-start.4 = (bf16[576,384]{1,0:T(8,128)(2,1)S(1)}, bf16[576,384]{1,0:T(8,128)(2,1)S(1)}, u32[]{:S(2)}, u32[]{:S(2)}) collective-permute-start(bf16[576,384]{1,0:T(8,128)(2,1)S(1)} %collective-permute-done.3), channel_id=1, source_target_pairs={{0,1},{1,2},{2,3},{3,0},{4,5},{5,6},{6,7},{7,4},{8,9},{9,10},{10,1... | collective-permute-start | bytes 1327112 | tf_op jit(solution)/shard_map/ppermute | solution.py:49
  41.1 1.0 copy-start.1
  41.2 1.7 copy-start.4
  42.4 1.1 copy-start.3
  43.5 13.3 %copy-start.2 = (bf16[1024,384]{1,0:T(8,128)(2,1)S(1)}, bf16[1024,384]{1,0:T(8,128)(2,1)}, u32[]{:S(2)}) copy-start(bf16[1024,384]{1,0:T(8,128)(2,1)} %param.4) | copy-start | bytes 2359300
  46.5 24.9 %collective-permute-start.6 = (bf16[1024,384]{0,1:T(8,128)(2,1)}, bf16[1024,384]{0,1:T(8,128)(2,1)}, u32[]{:S(2)}, u32[]{:S(2)}) collective-permute-start(bf16[1024,384]{0,1:T(8,128)(2,1)} %get-tuple-element.6), channel_id=1, source_target_pairs={{2,0},{3,1},{4,2},{5,3},{6,4},{7,5},{8,6},{9,7},{10,8},{11,9},{12,... | collective-permute-start | bytes 2359304 | tf_op jit(solution)/shard_map/ppermute | solution.py:14
  47.8 39.3 %collective-permute-start.5 = (bf16[1024,384]{0,1:T(8,128)(2,1)}, bf16[1024,384]{0,1:T(8,128)(2,1)}, u32[]{:S(2)}, u32[]{:S(2)}) collective-permute-start(bf16[1024,384]{0,1:T(8,128)(2,1)} %get-tuple-element.6), channel_id=1, source_target_pairs={{0,2},{1,3},{2,4},{3,5},{4,6},{5,7},{6,8},{7,9},{8,10},{9,11},{10,... | collective-permute-start | bytes 2359304 | tf_op jit(solution)/shard_map/ppermute | solution.py:14
  90.7 38.2 %collective-permute-start.8 = (bf16[1024,384]{0,1:T(8,128)(2,1)S(1)}, bf16[1024,384]{0,1:T(8,128)(2,1)S(1)}, u32[]{:S(2)}, u32[]{:S(2)}) collective-permute-start(bf16[1024,384]{0,1:T(8,128)(2,1)S(1)} %fusion), channel_id=1, source_target_pairs={{0,2},{1,3},{2,4},{3,5},{4,6},{5,7},{6,8},{7,9},{8,10},{9,11},{10,... | collective-permute-start | bytes 2359304 | tf_op jit(solution)/shard_map/ppermute | solution.py:14
  95.2 33.8 %collective-permute-start.7 = (bf16[1024,384]{0,1:T(8,128)(2,1)S(1)}, bf16[1024,384]{0,1:T(8,128)(2,1)S(1)}, u32[]{:S(2)}, u32[]{:S(2)}) collective-permute-start(bf16[1024,384]{0,1:T(8,128)(2,1)S(1)} %fusion), channel_id=1, source_target_pairs={{2,0},{3,1},{4,2},{5,3},{6,4},{7,5},{8,6},{9,7},{10,8},{11,9},{12,... | collective-permute-start | bytes 2359304 | tf_op jit(solution)/shard_map/ppermute | solution.py:14
  99.5 29.7 %copy-start.7 = (f32[1024,384]{0,1:T(8,128)S(1)}, f32[1024,384]{0,1:T(8,128)}, u32[]{:S(2)}) copy-start(f32[1024,384]{0,1:T(8,128)} %get-tuple-element.7) | copy-start | bytes 4718596
  129.2 3.1 %copy-start.5 = (bf16[1024,1152]{1,0:T(8,128)(2,1)S(1)}, bf16[1024,1152]{1,0:T(8,128)(2,1)}, u32[]{:S(2)}) copy-start(bf16[1024,1152]{1,0:T(8,128)(2,1)} %copy-done.4) | copy-start | bytes 7077892
  135.7 92.7 %all-reduce.2.cloned.1.call-start = ((), (), s32[]{:S(2)}) async-start(), calls=%async_computation.2 | async-start | bytes 1769472 | tf_op jit(solution)/shard_map/psum | solution.py:90
  135.8 41.9 %collective-permute-start.10 = (bf16[1024,384]{0,1:T(8,128)(2,1)S(1)}, bf16[1024,384]{0,1:T(8,128)(2,1)S(1)}, u32[]{:S(2)}, u32[]{:S(2)}) collective-permute-start(bf16[1024,384]{0,1:T(8,128)(2,1)S(1)} %get-tuple-element.8), channel_id=1, source_target_pairs={{0,1},{1,2},{2,3},{3,4},{4,5},{5,6},{6,7},{7,8},{8,9},{9,10},{10,1... | collective-permute-start | bytes 2359304 | tf_op jit(solution)/shard_map/ppermute | solution.py:14
  137.1 40.6 %collective-permute-start.9 = (bf16[1024,384]{0,1:T(8,128)(2,1)S(1)}, bf16[1024,384]{0,1:T(8,128)(2,1)S(1)}, u32[]{:S(2)}, u32[]{:S(2)}) collective-permute-start(bf16[1024,384]{0,1:T(8,128)(2,1)S(1)} %get-tuple-element.8), channel_id=1, source_target_pairs={{1,0},{2,1},{3,2},{4,3},{5,4},{6,5},{7,6},{8,7},{9,8},{10,9},{11,1... | collective-permute-start | bytes 2359304 | tf_op jit(solution)/shard_map/ppermute | solution.py:14
  177.6 1.4 copy-start.6
Sparse Core Ops, SparseCore 0:
  135.8 41.7 reduce-scatter.1
  180.1 48.2 all-reduce.1
